TPU v7x, 32 devices: a whole 2x2x4 slice. The times are simulated.
32 devices in a mesh: ctx: 8 (over y, x, core), fsdp: 4 (over z).
Axes of the slice: x: 2, y: 2, z: 4, core: 2. Of those that a mesh axis runs over, the one named last changes fastest.
Arguments:
- layer_in: bfloat16 [8, 1024, 1024], P('fsdp', 'ctx'), may hold values from -6 to 6
- block_order: int32 [8, 16], P('fsdp'), may hold values from 0 to 15, as said below
- ln1_gain: bfloat16 [1024], P('fsdp'), may hold values from 0.5 to 1.5
- ln1_shift: bfloat16 [1024], P('fsdp'), may hold values from -3 to 3
- w_qkv: bfloat16 [1024, 3072], P('fsdp'), may hold values from -0.1875 to 0.1875
- b_query: bfloat16 [1024], P('fsdp'), may hold values from -3 to 3
- b_value: bfloat16 [1024], P('fsdp'), may hold values from -3 to 3
- w_out: bfloat16 [1024, 1024], P('fsdp'), may hold values from -1 to 1
- b_out: bfloat16 [1024], P('fsdp'), may hold values from -2 to 2
- ln2_gain: bfloat16 [1024], P('fsdp'), may hold values from 0.5 to 1.5
- ln2_shift: bfloat16 [1024], P('fsdp'), may hold values from -3 to 3
- w_up: bfloat16 [1024, 4096], P('fsdp'), may hold values from -0.1875 to 0.1875
- b_up: bfloat16 [4096], P('fsdp'), may hold values from -3 to 3
- w_down: bfloat16 [4096, 1024], P('fsdp'), may hold values from -0.09375 to 0.09375
- b_down: bfloat16 [1024], P('fsdp'), may hold values from -3 to 3
- cotangent: bfloat16 [8, 1024, 1024], P('fsdp', 'ctx'), may hold values from -6 to 6
Outputs:
- layer_out: bfloat16 [8, 1024, 1024], P('fsdp', 'ctx')
- input_grad: bfloat16 [8, 1024, 1024], P('fsdp', 'ctx')
- grad_ln1_gain: float32 [1024], P(('ctx', 'fsdp'))
- grad_ln1_shift: float32 [1024], P(('ctx', 'fsdp'))
- grad_w_qkv: float32 [1024, 3072], P(('ctx', 'fsdp'))
- grad_b_query: float32 [1024], P(('ctx', 'fsdp'))
- grad_b_value: float32 [1024], P(('ctx', 'fsdp'))
- grad_w_out: float32 [1024, 1024], P(('ctx', 'fsdp'))
- grad_b_out: float32 [1024], P(('ctx', 'fsdp'))
- grad_ln2_gain: float32 [1024], P(('ctx', 'fsdp'))
- grad_ln2_shift: float32 [1024], P(('ctx', 'fsdp'))
- grad_w_up: float32 [1024, 4096], P(('ctx', 'fsdp'))
- grad_b_up: float32 [4096], P(('ctx', 'fsdp'))
- grad_w_down: float32 [4096, 1024], P(('ctx', 'fsdp'))
- grad_b_down: float32 [1024], P(('ctx', 'fsdp'))
Inputs may be any that keep to these rules, and one draw needn't show every extreme that they name: Stored block j of sequence s (rows j * 64 to (j + 1) * 64 - 1 as stored) holds block block_order[s, j] of the true order; each row is a permutation, and entry 2c + 1 is 15 minus entry 2c.
All inputs are finite; a program needn't handle non-finite values.
Results may differ from a plain program's by a relative error of at most 0.012.
Values may be sent and summed in bfloat16 or wider, within the bound.
A program may use at most 512 MiB of HBM per device.

v0:
```python
import math
import jax
import jax.numpy as jnp
from jax import lax
from jax.sharding import PartitionSpec as P

D = 1024
HEADS = 8
HEAD_DIM = 128
EPSILON = 1e-05
NEG_LARGE = -1e30
GELU_C = math.sqrt(2.0 / math.pi)
GELU_K = 0.044715


def gelu_tanh(values):
    inner = jnp.tanh(GELU_C * (values + GELU_K * values * values * values))
    return 0.5 * values * (1.0 + inner)


def gelu_slope(values):
    inner = jnp.tanh(GELU_C * (values + GELU_K * values * values * values))
    return 0.5 * (1.0 + inner) + 0.5 * values * (1.0 - inner * inner) * GELU_C * (
        1.0 + 3.0 * GELU_K * values * values
    )


def normalize(values, gain_vec, shift_vec):
    average = jnp.mean(values, axis=-1, keepdims=True)
    centered = values - average
    inv_dev = lax.rsqrt(jnp.mean(centered * centered, axis=-1, keepdims=True) + EPSILON)
    normed = centered * inv_dev
    return (normed * gain_vec + shift_vec, normed, inv_dev)


def normalize_back(grad, normed, inv_dev, gain_vec):
    scaled = grad * gain_vec
    return inv_dev * (
        scaled
        - jnp.mean(scaled, axis=-1, keepdims=True)
        - normed * jnp.mean(scaled * normed, axis=-1, keepdims=True)
    )


def token_positions(order_row, seq_len, half_rows):
    rows = jnp.arange(seq_len, dtype=jnp.int32)
    slots = jnp.arange(order_row.shape[0], dtype=jnp.int32)
    picked = jnp.sum(
        jnp.where((rows // half_rows)[:, None] == slots[None, :], order_row[None, :], 0), axis=1
    )
    return picked * half_rows + rows % half_rows


def block_probs(query_heads, key_heads, query_pos, key_pos, row_lse, scale):
    raw_scores = jnp.einsum(
        "qhd,khd->hqk", query_heads, key_heads, preferred_element_type=jnp.float32
    )
    allowed = (query_pos[:, None] >= key_pos[None, :])[None]
    shifted = jnp.where(allowed, raw_scores * scale - row_lse[:, :, None], NEG_LARGE)
    return jnp.where(allowed, jnp.exp(shifted), 0.0)


def score_grads(probs, grad_probs, row_delta, scale):
    return (probs * (grad_probs - row_delta[:, :, None]) * scale).astype(jnp.bfloat16)


def per_device(
    layer_in,
    block_order,
    ln1_gain,
    ln1_shift,
    w_qkv,
    b_query,
    b_value,
    w_out,
    b_out,
    ln2_gain,
    ln2_shift,
    w_up,
    b_up,
    w_down,
    b_down,
    cotangent,
):
    full = (
        lax.all_gather(ln1_gain, "fsdp", axis=0, tiled=True),
        lax.all_gather(ln1_shift, "fsdp", axis=0, tiled=True),
        lax.all_gather(w_qkv, "fsdp", axis=0, tiled=True),
        lax.all_gather(b_query, "fsdp", axis=0, tiled=True),
        lax.all_gather(b_value, "fsdp", axis=0, tiled=True),
        lax.all_gather(w_out, "fsdp", axis=0, tiled=True),
        lax.all_gather(b_out, "fsdp", axis=0, tiled=True),
        lax.all_gather(ln2_gain, "fsdp", axis=0, tiled=True),
        lax.all_gather(ln2_shift, "fsdp", axis=0, tiled=True),
        lax.all_gather(w_up, "fsdp", axis=0, tiled=True),
        lax.all_gather(b_up, "fsdp", axis=0, tiled=True),
        lax.all_gather(w_down, "fsdp", axis=0, tiled=True),
        lax.all_gather(b_down, "fsdp", axis=0, tiled=True),
    )
    qkv_full, out_full, up_full, down_full = (full[2], full[5], full[9], full[11])
    first_gain = full[0].astype(jnp.float32)
    first_shift = full[1].astype(jnp.float32)
    query_bias = full[3].astype(jnp.float32)
    value_bias = full[4].astype(jnp.float32)
    out_bias = full[6].astype(jnp.float32)
    second_gain = full[7].astype(jnp.float32)
    second_shift = full[8].astype(jnp.float32)
    up_bias = full[10].astype(jnp.float32)
    down_bias = full[12].astype(jnp.float32)
    micro = layer_in.shape[0]
    tokens = layer_in.shape[1]
    seq_len = tokens * lax.axis_size("ctx")
    half_rows = tokens // 2
    key_block = min(512, seq_len)
    blocks = seq_len // key_block
    scale = HEAD_DIM ** (-0.5)
    here = lax.axis_index("ctx")
    heads_shape = (blocks, key_block, HEADS, HEAD_DIM)
    totals = [jnp.zeros(item.shape, jnp.float32) for item in full]
    outputs_fwd = []
    outputs_grad = []
    for micro_step in range(micro):
        pos_all = token_positions(block_order[micro_step], seq_len, half_rows)
        pos_mine = lax.dynamic_slice_in_dim(pos_all, here * tokens, tokens)
        pos_blocks = pos_all.reshape(blocks, key_block)
        inputs = layer_in[micro_step].astype(jnp.float32)
        first_out, first_normed, first_inv = normalize(inputs, first_gain, first_shift)
        first_low = first_out.astype(jnp.bfloat16)
        projected = jnp.dot(first_low, qkv_full, preferred_element_type=jnp.float32)
        query_low = (projected[:, :D] + query_bias).astype(jnp.bfloat16)
        key_low = projected[:, D : 2 * D].astype(jnp.bfloat16)
        value_low = (projected[:, 2 * D :] + value_bias).astype(jnp.bfloat16)
        keys_all, values_all = (
            lax.all_gather(key_low, "ctx", axis=0, tiled=True),
            lax.all_gather(value_low, "ctx", axis=0, tiled=True),
        )
        query_heads = query_low.reshape(tokens, HEADS, HEAD_DIM)
        key_blocks = keys_all.reshape(heads_shape)
        value_blocks = values_all.reshape(heads_shape)

        def stats_step(carry, piece):
            run_max, run_sum = carry
            key_piece, key_pos = piece
            raw_scores = (
                jnp.einsum(
                    "qhd,khd->hqk", query_heads, key_piece, preferred_element_type=jnp.float32
                )
                * scale
            )
            allowed = (pos_mine[:, None] >= key_pos[None, :])[None]
            masked = jnp.where(allowed, raw_scores, NEG_LARGE)
            new_max = jnp.maximum(run_max, jnp.max(masked, axis=-1))
            weights = jnp.where(allowed, jnp.exp(masked - new_max[:, :, None]), 0.0)
            run_sum = run_sum * jnp.exp(run_max - new_max) + jnp.sum(weights, axis=-1)
            return ((new_max, run_sum), None)

        start_state = (
            jnp.full((HEADS, tokens), NEG_LARGE, jnp.float32),
            jnp.zeros((HEADS, tokens), jnp.float32),
        )
        (run_max, run_sum), unused = lax.scan(stats_step, start_state, (key_blocks, pos_blocks))
        row_lse = run_max + jnp.log(run_sum)

        def output_step(carry, piece):
            acc_low, acc_exact = carry
            key_piece, value_piece, key_pos = piece
            probs = block_probs(query_heads, key_piece, pos_mine, key_pos, row_lse, scale)
            acc_low = acc_low + jnp.einsum(
                "hqk,khd->hqd",
                probs.astype(jnp.bfloat16),
                value_piece,
                preferred_element_type=jnp.float32,
            )
            acc_exact = acc_exact + jnp.einsum(
                "hqk,khd->hqd",
                probs,
                value_piece.astype(jnp.float32),
                preferred_element_type=jnp.float32,
            )
            return ((acc_low, acc_exact), None)

        start_acc = (
            jnp.zeros((HEADS, tokens, HEAD_DIM), jnp.float32),
            jnp.zeros((HEADS, tokens, HEAD_DIM), jnp.float32),
        )
        (attn_heads, exact_heads), unused = lax.scan(
            output_step, start_acc, (key_blocks, value_blocks, pos_blocks)
        )
        attn_low = jnp.transpose(attn_heads, (1, 0, 2)).reshape(tokens, D).astype(jnp.bfloat16)
        resid = inputs + jnp.dot(attn_low, out_full, preferred_element_type=jnp.float32) + out_bias
        second_out, second_normed, second_inv = normalize(resid, second_gain, second_shift)
        second_low = second_out.astype(jnp.bfloat16)
        hidden = jnp.dot(second_low, up_full, preferred_element_type=jnp.float32) + up_bias
        active_low = gelu_tanh(hidden).astype(jnp.bfloat16)
        result = (
            resid + jnp.dot(active_low, down_full, preferred_element_type=jnp.float32) + down_bias
        )
        outputs_fwd.append(result.astype(jnp.bfloat16))
        grad_out = cotangent[micro_step]
        grad_outf = grad_out.astype(jnp.float32)
        term_down = jnp.einsum(
            "tf,td->fd", active_low, grad_out, preferred_element_type=jnp.float32
        )
        grad_active = jnp.einsum(
            "td,fd->tf", grad_out, down_full, preferred_element_type=jnp.float32
        )
        grad_hidden = (grad_active * gelu_slope(hidden)).astype(jnp.bfloat16)
        term_up = jnp.einsum(
            "td,tf->df", second_low, grad_hidden, preferred_element_type=jnp.float32
        )
        grad_second = jnp.einsum(
            "tf,df->td", grad_hidden, up_full, preferred_element_type=jnp.float32
        )
        grad_resid = grad_outf + normalize_back(grad_second, second_normed, second_inv, second_gain)
        grad_branch = grad_resid.astype(jnp.bfloat16)
        term_out = jnp.einsum(
            "td,te->de", attn_low, grad_branch, preferred_element_type=jnp.float32
        )
        grad_attn = jnp.einsum(
            "te,de->td", grad_branch, out_full, preferred_element_type=jnp.float32
        ).astype(jnp.bfloat16)
        grad_heads = grad_attn.reshape(tokens, HEADS, HEAD_DIM)
        row_delta = jnp.einsum("qhd,hqd->hq", grad_heads.astype(jnp.float32), exact_heads)

        def backward_step(grad_query, piece):
            key_piece, value_piece, key_pos = piece
            probs = block_probs(query_heads, key_piece, pos_mine, key_pos, row_lse, scale)
            grad_value = jnp.einsum(
                "hqk,qhd->khd",
                probs.astype(jnp.bfloat16),
                grad_heads,
                preferred_element_type=jnp.float32,
            )
            grad_probs = jnp.einsum(
                "qhd,khd->hqk", grad_heads, value_piece, preferred_element_type=jnp.float32
            )
            grad_scores = score_grads(probs, grad_probs, row_delta, scale)
            grad_query = grad_query + jnp.einsum(
                "hqk,khd->qhd", grad_scores, key_piece, preferred_element_type=jnp.float32
            )
            grad_key = jnp.einsum(
                "hqk,qhd->khd", grad_scores, query_heads, preferred_element_type=jnp.float32
            )
            rows_here = key_piece.shape[0]
            return (
                grad_query,
                jnp.concatenate(
                    [grad_key.reshape(rows_here, D), grad_value.reshape(rows_here, D)], axis=1
                ),
            )

        grad_query, key_terms = lax.scan(
            backward_step,
            jnp.zeros((tokens, HEADS, HEAD_DIM), jnp.float32),
            (key_blocks, value_blocks, pos_blocks),
        )
        key_sums = lax.psum_scatter(
            key_terms.reshape(seq_len, 2 * D), "ctx", scatter_dimension=0, tiled=True
        )
        grad_key_low = key_sums[:, :D].astype(jnp.bfloat16)
        grad_value_low = key_sums[:, D:].astype(jnp.bfloat16)
        grad_query_low = grad_query.reshape(tokens, D).astype(jnp.bfloat16)
        grad_projected = jnp.concatenate([grad_query_low, grad_key_low, grad_value_low], axis=1)
        term_qkv = jnp.einsum(
            "td,te->de", first_low, grad_projected, preferred_element_type=jnp.float32
        )
        grad_first = jnp.einsum(
            "te,de->td", grad_projected, qkv_full, preferred_element_type=jnp.float32
        )
        grad_input = grad_resid + normalize_back(grad_first, first_normed, first_inv, first_gain)
        outputs_grad.append(grad_input.astype(jnp.bfloat16))
        terms = (
            jnp.sum(grad_first * first_normed, axis=0),
            jnp.sum(grad_first, axis=0),
            term_qkv,
            jnp.sum(grad_query_low.astype(jnp.float32), axis=0),
            jnp.sum(grad_value_low.astype(jnp.float32), axis=0),
            term_out,
            jnp.sum(grad_branch.astype(jnp.float32), axis=0),
            jnp.sum(grad_second * second_normed, axis=0),
            jnp.sum(grad_second, axis=0),
            term_up,
            jnp.sum(grad_hidden.astype(jnp.float32), axis=0),
            term_down,
            jnp.sum(grad_outf, axis=0),
        )
        totals = [older + newer for older, newer in zip(totals, terms)]
    summed = (
        lax.psum_scatter(totals[0], ("ctx", "fsdp"), scatter_dimension=0, tiled=True),
        lax.psum_scatter(totals[1], ("ctx", "fsdp"), scatter_dimension=0, tiled=True),
        lax.psum_scatter(totals[2], ("ctx", "fsdp"), scatter_dimension=0, tiled=True),
        lax.psum_scatter(totals[3], ("ctx", "fsdp"), scatter_dimension=0, tiled=True),
        lax.psum_scatter(totals[4], ("ctx", "fsdp"), scatter_dimension=0, tiled=True),
        lax.psum_scatter(totals[5], ("ctx", "fsdp"), scatter_dimension=0, tiled=True),
        lax.psum_scatter(totals[6], ("ctx", "fsdp"), scatter_dimension=0, tiled=True),
        lax.psum_scatter(totals[7], ("ctx", "fsdp"), scatter_dimension=0, tiled=True),
        lax.psum_scatter(totals[8], ("ctx", "fsdp"), scatter_dimension=0, tiled=True),
        lax.psum_scatter(totals[9], ("ctx", "fsdp"), scatter_dimension=0, tiled=True),
        lax.psum_scatter(totals[10], ("ctx", "fsdp"), scatter_dimension=0, tiled=True),
        lax.psum_scatter(totals[11], ("ctx", "fsdp"), scatter_dimension=0, tiled=True),
        lax.psum_scatter(totals[12], ("ctx", "fsdp"), scatter_dimension=0, tiled=True),
    )
    return (
        jnp.stack(outputs_fwd),
        jnp.stack(outputs_grad),
        summed[0],
        summed[1],
        summed[2],
        summed[3],
        summed[4],
        summed[5],
        summed[6],
        summed[7],
        summed[8],
        summed[9],
        summed[10],
        summed[11],
        summed[12],
    )


def solution(mesh):
    placed = (
        P("fsdp", "ctx", None),
        P("fsdp", None),
        P("fsdp"),
        P("fsdp"),
        P("fsdp", None),
        P("fsdp"),
        P("fsdp"),
        P("fsdp", None),
        P("fsdp"),
        P("fsdp"),
        P("fsdp"),
        P("fsdp", None),
        P("fsdp"),
        P("fsdp", None),
        P("fsdp"),
        P("fsdp", "ctx", None),
    )
    return jax.shard_map(
        per_device,
        mesh=mesh,
        in_specs=placed,
        out_specs=(
            P("fsdp", "ctx", None),
            P("fsdp", "ctx", None),
            P(("ctx", "fsdp")),
            P(("ctx", "fsdp")),
            P(("ctx", "fsdp"), None),
            P(("ctx", "fsdp")),
            P(("ctx", "fsdp")),
            P(("ctx", "fsdp"), None),
            P(("ctx", "fsdp")),
            P(("ctx", "fsdp")),
            P(("ctx", "fsdp")),
            P(("ctx", "fsdp"), None),
            P(("ctx", "fsdp")),
            P(("ctx", "fsdp"), None),
            P(("ctx", "fsdp")),
        ),
        check_vma=False,
    )
```

profile of v0, /device:TPU:0, one launch (start us, length us, event | category | flops | bytes accessed | tf_op | source)
XLA Modules:
  0.0 1857.9 jit_solution(17294477554371182860)
XLA Ops:
  9.3 12.6 all-gather.1
  31.3 96.4 %all-gather.17.cloned.1.call-done = bf16[1024,3072]{1,0:T(8,128)(2,1)} async-done(((bf16[256,3072]{1,0:T(8,128)(2,1)}), bf16[1024,3072]{1,0:T(8,128)(2,1)}) %all-gather.17.cloned.1.call-update) | async-done | bytes 6291472 | tf_op jit(solution)/shard_map/all_gather | solution.py:88
  140.4 9.2 all-gather.2
  159.8 8.3 all-gather.6
  168.1 8.9 all-gather.5
  176.9 8.3 all-gather.4
  185.2 12.0 all_gather.63
  207.3 11.5 all-gather.21.cloned.1.call-done
  221.4 27.1 %all-gather.19.cloned.1.call-done = bf16[1024,1024]{1,0:T(8,128)(2,1)} async-done(((bf16[128,1024]{1,0:T(8,128)(2,1)}), bf16[1024,1024]{1,0:T(8,128)(2,1)}) %all-gather.19.cloned.1.call-update) | async-done | bytes 2097168 | tf_op jit(solution)/shard_map/all_gather | solution.py:134
  257.4 10.1 while.81
  282.7 13.1 all-gather.23.cloned.1.call-done
  299.8 146.0 %all-gather.25.cloned.1.call-done = bf16[1024,4096]{1,0:T(8,128)(2,1)} async-done(((bf16[256,4096]{1,0:T(8,128)(2,1)}), bf16[1024,4096]{1,0:T(8,128)(2,1)}) %all-gather.25.cloned.1.call-update) | async-done | bytes 8388624 | tf_op jit(solution)/shard_map/all_gather | solution.py:95
  451.9 143.4 %all-gather.27.cloned.1.call-done = bf16[4096,1024]{1,0:T(8,128)(2,1)} async-done(((bf16[1024,1024]{1,0:T(8,128)(2,1)}), bf16[4096,1024]{1,0:T(8,128)(2,1)}) %all-gather.27.cloned.1.call-update) | async-done | bytes 8388624 | tf_op jit(solution)/shard_map/all_gather | solution.py:97
  627.2 35.6 %while.83 = (s32[]{:T(128)}, f32[128,8,128]{0,2,1:T(8,128)S(1)}, f32[2,512,2048]{2,1,0:T(8,128)}, bf16[2,512,8,128]{3,1,2,0:T(8,128)(2,1)}, s32[128]{0:T(128)S(1...) while((s32[]{:T(128)}, f32[128,8,128]{0,2,1:T(8,128)S(1)}, ...), condition=%wide.region_32.33_spmd.clone, body=%wide.region_31.32_spmd.clone.sunk | while | flops 677183488 | bytes 60963544 | solution.py:252
  678.0 36.3 %while.82 = (s32[]{:T(128)}, f32[128,8,128]{0,2,1:T(8,128)S(1)}, f32[2,512,2048]{2,1,0:T(8,128)}, bf16[2,512,8,128]{3,1,2,0:T(8,128)(2,1)}, s32[128]{0:T(128)S(1...) while((s32[]{:T(128)}, f32[128,8,128]{0,2,1:T(8,128)S(1)}, ...), condition=%wide.region_25.26_spmd.clone, body=%wide.region_24.25_spmd.clone.sunk | while | flops 677183488 | bytes 53623516 | solution.py:252
  719.8 12.6 reduce-scatter.9.cloned.1.call-done
  733.7 73.7 %reduce-scatter.7.cloned.1.call-done = f32[128,2048]{1,0:T(8,128)} async-done(((f32[1024,2048]{1,0:T(8,128)}), f32[128,2048]{1,0:T(8,128)}) %reduce-scatter.7.cloned.1.call-update) | async-done | bytes 1048592 | tf_op jit(solution)/shard_map/reduce_scatter | solution.py:257
  822.4 9.1 convolution_add_fusion.4
  845.2 11.1 all-gather.7
  873.3 38.9 %all-reduce.9 = (f32[1024]{0:T(1024)S(1)}, f32[1024]{0:T(1024)S(1)}, f32[1024]{0:T(1024)S(1)}, f32[1024]{0:T(1024)S(1)}, f32[1024]{0:T(1024)S(1)}, /*index=5*/f3...) all-reduce(f32[1024]{0:T(1024)S(1)} %add.391, ...), channel_id=4, replica_groups=mesh['ctx'=8,'fsdp'=4] {'ctx','fsdp'}, use_global_device_ids=true, to_apply=%region_38.39.clone | all-reduce | flops 12288 | bytes 98304
  918.8 40.4 %reduce-scatter.13.cloned.1.call-done = f32[32,1024]{1,0:T(8,128)} async-done(((f32[1024,1024]{1,0:T(8,128)}), f32[32,1024]{1,0:T(8,128)}) %reduce-scatter.13.cloned.1.call-update) | async-done | bytes 131088 | tf_op jit(solution)/shard_map/reduce_scatter | solution.py:294
  959.2 160.6 %reduce-scatter.11.cloned.1.call-done = f32[32,3072]{1,0:T(8,128)} async-done(((f32[1024,3072]{1,0:T(8,128)}), f32[32,3072]{1,0:T(8,128)}) %reduce-scatter.11.cloned.1.call-update) | async-done | bytes 393232 | tf_op jit(solution)/shard_map/reduce_scatter | solution.py:291
  1119.8 366.4 %reduce-scatter.17.cloned.1.call-done = f32[128,1024]{1,0:T(8,128)} async-done(((f32[4096,1024]{1,0:T(8,128)}), f32[128,1024]{1,0:T(8,128)}) %reduce-scatter.17.cloned.1.call-update) | async-done | bytes 524304 | tf_op jit(solution)/shard_map/reduce_scatter | solution.py:300
  1486.1 365.0 %reduce-scatter.15.cloned.1.call-done = f32[32,4096]{1,0:T(8,128)} async-done(((f32[1024,4096]{1,0:T(8,128)}), f32[32,4096]{1,0:T(8,128)}) %reduce-scatter.15.cloned.1.call-update) | async-done | bytes 524304 | tf_op jit(solution)/shard_map/reduce_scatter | solution.py:298
  (479 shorter events, 283.9 us)
Async XLA Ops:
  7.2 120.5 %all-gather.17.cloned.1.call-start = ((), (), s32[]{:S(2)}) async-start(), calls=%async_computation.6 | async-start | bytes 7864320 | tf_op jit(solution)/shard_map/all_gather | solution.py:88
  7.9 191.5 %all-gather.29.cloned.1.call-start = ((), (), s32[]{:S(2)}) async-start(), calls=%async_computation.12 | async-start | bytes 2359296 | tf_op jit(solution)/shard_map/all_gather | solution.py:134
  21.9 127.7 %copy-start.50 = (f32[4,1,256]{2,1,0:T(1,128)}, f32[4,1,256]{2,1,0:T(1,128)S(1)}, u32[]{:S(2)}) copy-start(f32[4,1,256]{2,1,0:T(1,128)S(1)} %convert_element_type.245) | copy-start | bytes 12292
  29.7 119.9 %copy-start.48 = (f32[4,1,256]{2,1,0:T(1,128)}, f32[4,1,256]{2,1,0:T(1,128)S(1)}, u32[]{:S(2)}) copy-start(f32[4,1,256]{2,1,0:T(1,128)S(1)} %convert_element_type.244) | copy-start | bytes 12292
  132.3 71.0 %all-gather.31.cloned.1.call-start = ((), (), s32[]{:S(2)}) async-start(), calls=%async_computation.13 | async-start | bytes 2359296 | tf_op jit(solution)/shard_map/all_gather | solution.py:135
  155.0 63.8 %all-gather.21.cloned.1.call-start = ((), (), s32[]{:S(2)}) async-start(), calls=%async_computation.8 | async-start | bytes 2359296 | tf_op jit(solution)/shard_map/all_gather | solution.py:135
  155.5 92.9 %all-gather.19.cloned.1.call-start = ((), (), s32[]{:S(2)}) async-start(), calls=%async_computation.7 | async-start | bytes 2359296 | tf_op jit(solution)/shard_map/all_gather | solution.py:134
  157.4 138.4 %all-gather.23.cloned.1.call-start = ((), (), s32[]{:S(2)}) async-start(), calls=%async_computation.9 | async-start | bytes 2621440 | tf_op jit(solution)/shard_map/all_gather | solution.py:91
  158.0 287.7 %all-gather.25.cloned.1.call-start = ((), (), s32[]{:S(2)}) async-start(), calls=%async_computation.10 | async-start | bytes 10485760 | tf_op jit(solution)/shard_map/all_gather | solution.py:95
  158.8 436.4 %all-gather.27.cloned.1.call-start = ((), (), s32[]{:S(2)}) async-start(), calls=%async_computation.11 | async-start | bytes 10485760 | tf_op jit(solution)/shard_map/all_gather | solution.py:97
  159.5 572.9 %reduce-scatter.9.cloned.1.call-start = ((), (), s32[]{:S(2)}) async-start(), calls=%async_computation.15 | async-start | bytes 9437184 | tf_op jit(solution)/shard_map/reduce_scatter | solution.py:257
  168.1 439.4 %copy-start.52 = (f32[4,1,256]{2,1,0:T(1,128)}, f32[4,1,256]{2,1,0:T(1,128)S(1)}, u32[]{:S(2)}) copy-start(f32[4,1,256]{2,1,0:T(1,128)S(1)} %convert_element_type.250) | copy-start | bytes 12292
  176.9 440.7 %copy-start.46 = (f32[4,1,256]{2,1,0:T(1,128)}, f32[4,1,256]{2,1,0:T(1,128)S(1)}, u32[]{:S(2)}) copy-start(f32[4,1,256]{2,1,0:T(1,128)S(1)} %convert_element_type.249) | copy-start | bytes 12292
  298.2 319.4 %copy-start.59 = (f32[128]{0:T(128)}, f32[128]{0:T(128)S(1)}, u32[]{:S(2)}) copy-start(f32[128]{0:T(128)S(1)} %broadcast_multiply_fusion.12) | copy-start | bytes 1540
  299.5 318.1 %copy-start.7 = (f32[128,1024]{1,0:T(8,128)}, f32[128,1024]{1,0:T(8,128)S(1)}, u32[]{:S(2)}) copy-start(f32[128,1024]{1,0:T(8,128)S(1)} %get-tuple-element.894) | copy-start | bytes 1572868
  299.6 318.1 %copy-start.61 = (f32[128]{0:T(128)}, f32[128]{0:T(128)S(1)}, u32[]{:S(2)}) copy-start(f32[128]{0:T(128)S(1)} %broadcast_multiply_fusion.10) | copy-start | bytes 1540
  299.8 317.9 %copy-start.67 = (f32[128]{0:T(128)}, f32[128]{0:T(128)S(1)}, u32[]{:S(2)}) copy-start(f32[128]{0:T(128)S(1)} %add_rsqrt_fusion.2) | copy-start | bytes 1540
  299.8 317.9 %copy-start.65 = (f32[128]{0:T(128)}, f32[128]{0:T(128)S(1)}, u32[]{:S(2)}) copy-start(f32[128]{0:T(128)S(1)} %add_rsqrt_fusion) | copy-start | bytes 1540
  445.8 149.5 %copy-start.45 = (bf16[2,128,1024]{2,1,0:T(8,128)(2,1)S(1)}, bf16[2,128,1024]{2,1,0:T(8,128)(2,1)}, u32[]{:S(2)}) copy-start(bf16[2,128,1024]{2,1,0:T(8,128)(2,1)} %param.43) | copy-start | bytes 1572868
  662.8 144.7 %reduce-scatter.7.cloned.1.call-start = ((), (), s32[]{:S(2)}) async-start(), calls=%async_computation.14 | async-start | bytes 9437184 | tf_op jit(solution)/shard_map/reduce_scatter | solution.py:257
  714.4 244.8 %reduce-scatter.13.cloned.1.call-start = ((), (), s32[]{:S(2)}) async-start(), calls=%async_computation.17 | async-start | bytes 4325376 | tf_op jit(solution)/shard_map/reduce_scatter | solution.py:294
  719.0 400.8 %reduce-scatter.11.cloned.1.call-start = ((), (), s32[]{:S(2)}) async-start(), calls=%async_computation.16 | async-start | bytes 12976128 | tf_op jit(solution)/shard_map/reduce_scatter | solution.py:291
  818.0 668.2 %reduce-scatter.17.cloned.1.call-start = ((), (), s32[]{:S(2)}) async-start(), calls=%async_computation.19 | async-start | bytes 17301504 | tf_op jit(solution)/shard_map/reduce_scatter | solution.py:300
  831.6 1019.5 %reduce-scatter.15.cloned.1.call-start = ((), (), s32[]{:S(2)}) async-start(), calls=%async_computation.18 | async-start | bytes 17301504 | tf_op jit(solution)/shard_map/reduce_scatter | solution.py:298
  (97 other events, 1500.8 us)
Sparse Core Ops, SparseCore 0:
  9.6 118.0 all-gather.16
  132.5 26.1 all-gather.28
  161.2 27.8 all-gather.30
  190.8 27.8 all-gather.20
  220.5 27.8 all-gather.18
  249.8 45.9 all-gather.22
  297.4 148.3 all-gather.24
  447.3 147.8 all-gather.26
  662.9 69.4 reduce-scatter.8
  736.1 71.2 reduce-scatter.6
  810.3 148.8 reduce-scatter.12
  965.6 154.0 reduce-scatter.10
  1122.7 363.3 reduce-scatter.16
  1488.9 362.1 reduce-scatter.14
where the time goes:
time: 1860 us
  waiting for transfers between devices  1460 us (78%)
  matrix products  130 us (7%)
  blocking collectives  125 us (7%)
  local copies, waits for them, and re-layouts  97.7 us (5%)
  other arithmetic  28.4 us (2%)
    reduce_scatter x1, waiting for transfers between devices, per_device(): lax.psum_scatter(totals[11], ('ctx', 'fsdp'), scatter_dimension=0, tiled=...  366 us
    reduce_scatter x1, waiting for transfers between devices, per_device(): lax.psum_scatter(totals[9], ('ctx', 'fsdp'), scatter_dimension=0, tiled=T...  365 us
    reduce_scatter x1, waiting for transfers between devices, per_device(): lax.psum_scatter(totals[2], ('ctx', 'fsdp'), scatter_dimension=0, tiled=T...  161 us
    all_gather x1, waiting for transfers between devices, per_device(): lax.all_gather(w_up, 'fsdp', axis=0, tiled=True)  146 us
    all_gather x1, waiting for transfers between devices, per_device(): lax.all_gather(w_down, 'fsdp', axis=0, tiled=True)  143 us
    all_gather x1, waiting for transfers between devices, per_device(): lax.all_gather(w_qkv, 'fsdp', axis=0, tiled=True)  96.4 us
    reduce_scatter x2, waiting for transfers between devices, per_device(): lax.psum_scatter(key_terms.reshape(seq_len, 2 * D), 'ctx', scatter_dimens...  86.3 us
    dynamic_update_slice x8, local copies, waits for them, and re-layouts, per_device(): lax.scan(backward_step, jnp.zeros((tokens, HEADS, HEAD_DIM), jnp.float32)...  41 us
  transfers between devices with their start and end apart: 14, of which 12 were waited for; matrix products, arithmetic and copies ran while one was open for 9% of the time, Pallas kernels for 0%

commit v1 on v0

--- a/solution.py
+++ b/solution.py
@@ -11,6 +11,28 @@
 NEG_LARGE = -1e30
 GELU_C = math.sqrt(2.0 / math.pi)
 GELU_K = 0.044715
+
+
+def laid_out(blocks, dim):
+    blocks = jnp.moveaxis(blocks, 0, dim)
+    shape = blocks.shape
+    return blocks.reshape(*shape[:dim], shape[dim] * shape[dim + 1], *shape[dim + 2 :])
+
+
+def doubled(shard, axis):
+    size = lax.axis_size(axis)
+    blocks = shard[None]
+    for level in range(size.bit_length() - 1):
+        bit = 1 << level
+        other = lax.ppermute(blocks, axis, [(i, i ^ bit) for i in range(size)])
+        both = jnp.stack([blocks, other])
+        upper = lax.axis_index(axis) >> level & 1
+        blocks = jnp.where(upper == 0, both, both[::-1]).reshape(-1, *shard.shape)
+    return blocks
+
+
+def collect(x, axis, dim):
+    return laid_out(doubled(x, axis), dim)
 
 
 def gelu_tanh(values):
@@ -92,7 +114,7 @@
         lax.all_gather(b_out, "fsdp", axis=0, tiled=True),
         lax.all_gather(ln2_gain, "fsdp", axis=0, tiled=True),
         lax.all_gather(ln2_shift, "fsdp", axis=0, tiled=True),
-        lax.all_gather(w_up, "fsdp", axis=0, tiled=True),
+        collect(w_up, "fsdp", 0),
         lax.all_gather(b_up, "fsdp", axis=0, tiled=True),
         lax.all_gather(w_down, "fsdp", axis=0, tiled=True),
         lax.all_gather(b_down, "fsdp", axis=0, tiled=True),

time: 1860 us -> 1930 us (1.038)
  blocking collectives: 125 us -> 458 us
  waiting for transfers between devices: 1460 us -> 1160 us
  other arithmetic: 28.4 us -> 56.3 us
    all_gather x1, blocking collectives: 8.86 us -> 241 us  [per_device(): lax.all_gather(ln2_gain, 'fsdp', axis=0, tiled=True)]
    all_gather x1 -> x0, waiting for transfers between devices: 146 us -> none  [per_device(): lax.all_gather(w_up, 'fsdp', axis=0, tiled=True)]
    all_gather x1, waiting for transfers between devices: 143 us -> 0.01 us  [per_device(): lax.all_gather(w_down, 'fsdp', axis=0, tiled=True)]
    all_gather x1, blocking collectives: 8.29 us -> 110 us  [per_device(): lax.all_gather(ln2_shift, 'fsdp', axis=0, tiled=True)]
    ppermute x0 -> x2, waiting for transfers between devices: none -> 43.3 us  [doubled(): other = lax.ppermute(blocks, axis, [(i, i ^ bit) for i in range(size)])]
    all_gather x2, waiting for transfers between devices: 27.1 us -> 0.04 us  [per_device(): lax.all_gather(key_low, 'ctx', axis=0, tiled=True)]
  transfers between devices with their start and end apart: 14 -> 15, of which waited for: 12 -> 8; matrix products, arithmetic and copies ran while one was open for 9% -> 10% of each run, Pallas kernels for 0% -> 0%
where the time goes in v1:
time: 1930 us
  waiting for transfers between devices  1160 us (60%)
  blocking collectives  458 us (24%)
  matrix products  136 us (7%)
  local copies, waits for them, and re-layouts  96.3 us (5%)
  other arithmetic  56.3 us (3%)
    reduce_scatter x1, waiting for transfers between devices, per_device(): lax.psum_scatter(totals[11], ('ctx', 'fsdp'), scatter_dimension=0, tiled=...  366 us
    reduce_scatter x1, waiting for transfers between devices, per_device(): lax.psum_scatter(totals[9], ('ctx', 'fsdp'), scatter_dimension=0, tiled=T...  365 us
    all_gather x1, blocking collectives, per_device(): lax.all_gather(ln2_gain, 'fsdp', axis=0, tiled=True)  241 us
    reduce_scatter x1, waiting for transfers between devices, per_device(): lax.psum_scatter(totals[2], ('ctx', 'fsdp'), scatter_dimension=0, tiled=T...  161 us
    all_gather x1, blocking collectives, per_device(): lax.all_gather(ln2_shift, 'fsdp', axis=0, tiled=True)  110 us
    all_gather x1, waiting for transfers between devices, per_device(): lax.all_gather(w_qkv, 'fsdp', axis=0, tiled=True)  96.4 us
    reduce_scatter x2, waiting for transfers between devices, per_device(): lax.psum_scatter(key_terms.reshape(seq_len, 2 * D), 'ctx', scatter_dimens...  86.2 us
    ppermute x2, waiting for transfers between devices, doubled(): other = lax.ppermute(blocks, axis, [(i, i ^ bit) for i in range(size)])  43.3 us
  transfers between devices with their start and end apart: 15, of which 8 were waited for; matrix products, arithmetic and copies ran while one was open for 10% of the time, Pallas kernels for 0%

profile of v1, /device:TPU:0, one launch (start us, length us, event | category | flops | bytes accessed | tf_op | source)
XLA Modules:
  0.0 1926.0 jit_solution(17465133771471344634)
XLA Ops:
  9.3 12.6 all-gather.1
  21.9 7.8 all-gather
  31.3 96.4 %all-gather.16.cloned.1.call-done = bf16[1024,3072]{1,0:T(8,128)(2,1)} async-done(((bf16[256,3072]{1,0:T(8,128)(2,1)}), bf16[1024,3072]{1,0:T(8,128)(2,1)}) %all-gather.16.cloned.1.call-update) | async-done | bytes 6291472 | tf_op jit(solution)/shard_map/all_gather | solution.py:110
  132.4 7.9 all-gather.3
  140.4 9.2 all-gather.2
  158.5 43.3 %collective-permute-done = bf16[1,256,4096]{2,1,0:T(8,128)(2,1)S(1)} collective-permute-done((bf16[1,256,4096]{2,1,0:T(8,128)(2,1)}, bf16[1,256,4096]{2,1,0:T(8,128)(2,1)S(1)}, u32[]{:S(2)}, u32[]{:S(2)}) %collective-permute-start) | collective-permute-done | bytes 2097184 | tf_op jit(solution)/shard_map/ppermute | solution.py:27
  209.2 110.4 %all-gather.6 = bf16[4,1,256]{2,1,0:T(2,128)(2,1)S(1)} all-gather(bf16[1,1,256]{2,1,0:T(2,128)(2,1)S(1)} %reshape.399), channel_id=1, replica_groups=mesh['ctx'=8,'fsdp'=4] {'fsdp'}, dimensions={0}, use_global_device_ids=true | all-gather | bytes 2560 | tf_op jit(solution)/shard_map/all_gather | solution.py:116
  319.6 240.7 %all-gather.5 = bf16[4,1,256]{2,1,0:T(2,128)(2,1)S(1)} all-gather(bf16[1,1,256]{2,1,0:T(2,128)(2,1)S(1)} %reshape.397), channel_id=1, replica_groups=mesh['ctx'=8,'fsdp'=4] {'fsdp'}, dimensions={0}, use_global_device_ids=true | all-gather | bytes 2560 | tf_op jit(solution)/shard_map/all_gather | solution.py:115
  568.0 12.2 all_gather.59
  587.9 13.6 reverse_select_fusion
  623.3 10.0 while.81
  658.5 8.1 convert_reduce_fusion
  696.7 35.4 %while.83 = (s32[]{:T(128)}, f32[128,8,128]{0,2,1:T(8,128)S(1)}, f32[2,512,2048]{2,1,0:T(8,128)}, bf16[2,512,8,128]{3,1,2,0:T(8,128)(2,1)}, s32[128]{0:T(128)S(1...) while((s32[]{:T(128)}, f32[128,8,128]{0,2,1:T(8,128)S(1)}, ...), condition=%wide.region_32.33_spmd.clone, body=%wide.region_31.32_spmd.clone.sunk | while | flops 677183488 | bytes 60963544 | solution.py:274
  747.0 36.1 %while.82 = (s32[]{:T(128)}, f32[128,8,128]{0,2,1:T(8,128)S(1)}, f32[2,512,2048]{2,1,0:T(8,128)}, bf16[2,512,8,128]{3,1,2,0:T(8,128)(2,1)}, s32[128]{0:T(128)S(1...) while((s32[]{:T(128)}, f32[128,8,128]{0,2,1:T(8,128)S(1)}, ...), condition=%wide.region_25.26_spmd.clone, body=%wide.region_24.25_spmd.clone.sunk | while | flops 677183488 | bytes 53623516 | solution.py:274
  788.6 12.4 reduce-scatter.9.cloned.1.call-done
  802.3 73.9 %reduce-scatter.7.cloned.1.call-done = f32[128,2048]{1,0:T(8,128)} async-done(((f32[1024,2048]{1,0:T(8,128)}), f32[128,2048]{1,0:T(8,128)}) %reduce-scatter.7.cloned.1.call-update) | async-done | bytes 1048592 | tf_op jit(solution)/shard_map/reduce_scatter | solution.py:279
  891.1 9.1 convolution_add_fusion.4
  905.0 8.2 convolution_add_fusion.5
  913.9 11.1 all-gather.7
  941.9 38.1 %all-reduce.9 = (f32[1024]{0:T(1024)S(1)}, f32[1024]{0:T(1024)S(1)}, f32[1024]{0:T(1024)S(1)}, f32[1024]{0:T(1024)S(1)}, f32[1024]{0:T(1024)S(1)}, /*index=5*/f3...) all-reduce(f32[1024]{0:T(1024)S(1)} %add.391, ...), channel_id=4, replica_groups=mesh['ctx'=8,'fsdp'=4] {'ctx','fsdp'}, use_global_device_ids=true, to_apply=%region_38.39.clone | all-reduce | flops 12288 | bytes 98304
  986.6 40.4 %reduce-scatter.13.cloned.1.call-done = f32[32,1024]{1,0:T(8,128)} async-done(((f32[1024,1024]{1,0:T(8,128)}), f32[32,1024]{1,0:T(8,128)}) %reduce-scatter.13.cloned.1.call-update) | async-done | bytes 131088 | tf_op jit(solution)/shard_map/reduce_scatter | solution.py:316
  1027.0 160.9 %reduce-scatter.11.cloned.1.call-done = f32[32,3072]{1,0:T(8,128)} async-done(((f32[1024,3072]{1,0:T(8,128)}), f32[32,3072]{1,0:T(8,128)}) %reduce-scatter.11.cloned.1.call-update) | async-done | bytes 393232 | tf_op jit(solution)/shard_map/reduce_scatter | solution.py:313
  1187.9 366.2 %reduce-scatter.17.cloned.1.call-done = f32[128,1024]{1,0:T(8,128)} async-done(((f32[4096,1024]{1,0:T(8,128)}), f32[128,1024]{1,0:T(8,128)}) %reduce-scatter.17.cloned.1.call-update) | async-done | bytes 524304 | tf_op jit(solution)/shard_map/reduce_scatter | solution.py:322
  1554.1 365.2 %reduce-scatter.15.cloned.1.call-done = f32[32,4096]{1,0:T(8,128)} async-done(((f32[1024,4096]{1,0:T(8,128)}), f32[32,4096]{1,0:T(8,128)}) %reduce-scatter.15.cloned.1.call-update) | async-done | bytes 524304 | tf_op jit(solution)/shard_map/reduce_scatter | solution.py:320
  (491 shorter events, 278.6 us)
Async XLA Ops:
  7.2 120.5 %all-gather.16.cloned.1.call-start = ((), (), s32[]{:S(2)}) async-start(), calls=%async_computation.6 | async-start | bytes 7864320 | tf_op jit(solution)/shard_map/all_gather | solution.py:110
  7.9 595.4 %all-gather.26.cloned.1.call-start = ((), (), s32[]{:S(2)}) async-start(), calls=%async_computation.11 | async-start | bytes 2359296 | tf_op jit(solution)/shard_map/all_gather | solution.py:156
  21.9 127.7 %copy-start.49 = (f32[4,1,256]{2,1,0:T(1,128)}, f32[4,1,256]{2,1,0:T(1,128)S(1)}, u32[]{:S(2)}) copy-start(f32[4,1,256]{2,1,0:T(1,128)S(1)} %convert_element_type.245) | copy-start | bytes 12292
  29.7 119.9 %copy-start.47 = (f32[4,1,256]{2,1,0:T(1,128)}, f32[4,1,256]{2,1,0:T(1,128)S(1)}, u32[]{:S(2)}) copy-start(f32[4,1,256]{2,1,0:T(1,128)S(1)} %convert_element_type.244) | copy-start | bytes 12292
  30.9 100.7 %copy-start.58 = (f32[128]{0:T(128)}, f32[128]{0:T(128)S(1)}, u32[]{:S(2)}) copy-start(f32[128]{0:T(128)S(1)} %get-tuple-element.907) | copy-start | bytes 1540
  30.9 118.7 %copy-start.64 = (f32[128]{0:T(128)}, f32[128]{0:T(128)S(1)}, u32[]{:S(2)}) copy-start(f32[128]{0:T(128)S(1)} %get-tuple-element.908) | copy-start | bytes 1540
  31.2 100.3 %copy-start.80 = (f32[128]{0:T(128)}, f32[128]{0:T(128)S(1)}, u32[]{:S(2)}) copy-start(f32[128]{0:T(128)S(1)} %add_rsqrt_fusion.1) | copy-start | bytes 1540
  132.4 474.9 %all-gather.28.cloned.1.call-start = ((), (), s32[]{:S(2)}) async-start(), calls=%async_computation.12 | async-start | bytes 2359296 | tf_op jit(solution)/shard_map/all_gather | solution.py:157
  155.2 456.0 %all-gather.20.cloned.1.call-start = ((), (), s32[]{:S(2)}) async-start(), calls=%async_computation.8 | async-start | bytes 2359296 | tf_op jit(solution)/shard_map/all_gather | solution.py:157
  155.8 458.0 %all-gather.18.cloned.1.call-start = ((), (), s32[]{:S(2)}) async-start(), calls=%async_computation.7 | async-start | bytes 2359296 | tf_op jit(solution)/shard_map/all_gather | solution.py:156
  157.6 490.8 %all-gather.22.cloned.1.call-start = ((), (), s32[]{:S(2)}) async-start(), calls=%async_computation.9 | async-start | bytes 2621440 | tf_op jit(solution)/shard_map/all_gather | solution.py:113
  157.7 44.1 %collective-permute-start = (bf16[1,256,4096]{2,1,0:T(8,128)(2,1)}, bf16[1,256,4096]{2,1,0:T(8,128)(2,1)S(1)}, u32[]{:S(2)}, u32[]{:S(2)}) collective-permute-start(bf16[1,256,4096]{2,1,0:T(8,128)(2,1)} %bitcast.491), channel_id=1, source_target_pairs={{0,1},{1,0},{2,3},{3,2},{4,5},{5,4},{6,7},{7,6},{8,9},{9,8},{10,11... | collective-permute-start | bytes 6291464 | tf_op jit(solution)/shard_map/ppermute | solution.py:27
  158.5 500.0 %all-gather.24.cloned.1.call-start = ((), (), s32[]{:S(2)}) async-start(), calls=%async_computation.10 | async-start | bytes 10485760 | tf_op jit(solution)/shard_map/all_gather | solution.py:119
  208.4 359.5 %copy-start.85 = (bf16[1024]{0:T(1024)(128)(2,1)S(1)}, bf16[1024]{0:T(1024)(128)(2,1)}, u32[]{:S(2)}) copy-start(bf16[1024]{0:T(1024)(128)(2,1)} %param.40) | copy-start | bytes 6148
  208.4 371.7 %copy-start.86 = (s32[2,16]{1,0:T(2,128)S(1)}, s32[2,16]{1,0:T(2,128)}, u32[]{:S(2)}) copy-start(s32[2,16]{1,0:T(2,128)} %param.29) | copy-start | bytes 388
  208.5 372.0 %collective-permute-start.1 = (bf16[2,256,4096]{2,1,0:T(8,128)(2,1)}, bf16[2,256,4096]{2,1,0:T(8,128)(2,1)}, u32[]{:S(2)}, u32[]{:S(2)}) collective-permute-start(bf16[2,256,4096]{2,1,0:T(8,128)(2,1)} %get-tuple-element.867), channel_id=1, source_target_pairs={{0,2},{1,3},{2,0},{3,1},{4,6},{5,7},{6,4},{7,5},{8,10},{9,11},{10,... | collective-permute-start | bytes 12582920 | tf_op jit(solution)/shard_map/ppermute | solution.py:27
  209.0 592.0 %reduce-scatter.9.cloned.1.call-start = ((), (), s32[]{:S(2)}) async-start(), calls=%async_computation.14 | async-start | bytes 9437184 | tf_op jit(solution)/shard_map/reduce_scatter | solution.py:279
  319.6 354.5 %copy-start.51 = (f32[4,1,256]{2,1,0:T(1,128)}, f32[4,1,256]{2,1,0:T(1,128)S(1)}, u32[]{:S(2)}) copy-start(f32[4,1,256]{2,1,0:T(1,128)S(1)} %convert_element_type.250) | copy-start | bytes 12292
  560.4 126.7 %copy-start.45 = (f32[4,1,256]{2,1,0:T(1,128)}, f32[4,1,256]{2,1,0:T(1,128)S(1)}, u32[]{:S(2)}) copy-start(f32[4,1,256]{2,1,0:T(1,128)S(1)} %convert_element_type.249) | copy-start | bytes 12292
  732.1 144.0 %reduce-scatter.7.cloned.1.call-start = ((), (), s32[]{:S(2)}) async-start(), calls=%async_computation.13 | async-start | bytes 9437184 | tf_op jit(solution)/shard_map/reduce_scatter | solution.py:279
  783.2 243.8 %reduce-scatter.13.cloned.1.call-start = ((), (), s32[]{:S(2)}) async-start(), calls=%async_computation.16 | async-start | bytes 4325376 | tf_op jit(solution)/shard_map/reduce_scatter | solution.py:316
  787.8 400.1 %reduce-scatter.11.cloned.1.call-start = ((), (), s32[]{:S(2)}) async-start(), calls=%async_computation.15 | async-start | bytes 12976128 | tf_op jit(solution)/shard_map/reduce_scatter | solution.py:313
  886.7 667.4 %reduce-scatter.17.cloned.1.call-start = ((), (), s32[]{:S(2)}) async-start(), calls=%async_computation.18 | async-start | bytes 17301504 | tf_op jit(solution)/shard_map/reduce_scatter | solution.py:322
  900.3 1019.0 %reduce-scatter.15.cloned.1.call-start = ((), (), s32[]{:S(2)}) async-start(), calls=%async_computation.17 | async-start | bytes 17301504 | tf_op jit(solution)/shard_map/reduce_scatter | solution.py:320
  (101 other events, 1361.9 us)
Sparse Core Ops, SparseCore 0:
  9.6 118.0 all-gather.15
  132.5 26.1 all-gather.25
  160.6 27.8 all-gather.27
  190.3 27.8 all-gather.19
  219.9 27.8 all-gather.17
  249.3 98.9 all-gather.21
  349.9 206.7 all-gather.23
  732.3 68.6 reduce-scatter.8
  804.9 71.2 reduce-scatter.6
  878.9 148.1 reduce-scatter.12
  1033.6 154.2 reduce-scatter.10
  1190.7 363.3 reduce-scatter.16
  1557.0 362.1 reduce-scatter.14
